TPU v7x, 256 devices: a whole 4x4x8 slice. The times are simulated.
256 devices in a mesh: orb: 16 (over y, x), aux: 16 (over z, core).
Axes of the slice: x: 4, y: 4, z: 8, core: 2. Of those that a mesh axis runs over, the one named last changes fastest.
Arguments:
- b_rows: bfloat16 [4096, 128, 8, 128], P('aux', 'orb'), may hold values from -6 to 6
- col_blocks: int32 [16, 8], P('orb'), may hold values from 0 to 15, all different within a row
- g_occ: bfloat16 [2, 128, 128], P(None, 'orb'), may hold values from -0.5 to 0.5
- occ_live: int32 [2, 16, 16], replicated, may hold values 0 or 1
- g_virt: bfloat16 [2, 16, 128, 128], P(None, 'orb', 'aux'), may hold values from -0.5 to 0.5
- tau_weight: float32 [2], replicated, may hold values from 0.5 to 2
Outputs:
- chi: float32 [256, 4096], P('orb', 'aux')
Inputs may be any that keep to these rules, and one draw needn't show every extreme that they name: `col_blocks`: each row group lists 8 different column blocks, and every column block is listed by some row group.
All inputs are finite; a program needn't handle non-finite values.
Results may differ from a plain program's by a relative error of at most 0.0041.
Values may be sent and summed in bfloat16 or wider, within the bound.
A program may use at most 128 MiB of HBM per device.

v0:
```python
import math
import jax
import jax.numpy as jnp
from jax import lax
from jax.sharding import PartitionSpec as P


def on_device(b_rows, col_blocks, g_occ, occ_live, g_virt, tau_weight):
    orb_count = lax.axis_size("orb")
    aux_dev, rows_dev, slot_count, tile_width = b_rows.shape
    tau_count = g_occ.shape[0]
    picked = (col_blocks[0][:, None] == jnp.arange(orb_count, dtype=jnp.int32)[None, :]).astype(
        jnp.bfloat16
    )
    outgoing = jnp.einsum("prkc,kd->prdc", b_rows, picked)
    occ_full = lax.all_gather(g_occ, "orb", axis=1, tiled=True)
    total_rows = occ_full.shape[1]
    live_mask = jnp.repeat(jnp.repeat(occ_live, rows_dev, axis=1), rows_dev, axis=2).astype(
        jnp.bfloat16
    )
    occ_masked = occ_full * live_mask
    virt_block = lax.all_gather(g_virt, "aux", axis=2, tiled=True)
    col_dense = lax.all_to_all(outgoing, "orb", split_axis=2, concat_axis=1, tiled=True).reshape(
        aux_dev, total_rows, tile_width
    )
    virt_list = []
    for moment in range(tau_count):
        product = jnp.dot(
            col_dense.reshape(aux_dev * total_rows, tile_width),
            virt_block[moment, 0],
            preferred_element_type=jnp.float32,
        )
        virt_list.append(product.astype(jnp.bfloat16).reshape(aux_dev, total_rows, tile_width))
    partial_value = jnp.zeros((aux_dev, aux_dev), jnp.float32)
    for moment in range(tau_count):
        occ_prod = jnp.einsum(
            "mn,qnc->qmc", occ_masked[moment], col_dense, preferred_element_type=jnp.float32
        ).astype(jnp.bfloat16)
        term = jnp.einsum(
            "pmc,qmc->qp", virt_list[moment], occ_prod, preferred_element_type=jnp.float32
        )
        partial_value = partial_value + tau_weight[moment] * term
    partial_value = partial_value * (1.0 / math.sqrt(total_rows * tile_width * orb_count))
    whole_sum = lax.psum(partial_value, "orb")
    share_rows = aux_dev // orb_count
    share = lax.dynamic_slice_in_dim(whole_sum, lax.axis_index("orb") * share_rows, share_rows, 0)
    return share


def solution(mesh):
    in_specs = (
        P("aux", "orb", None, None),
        P("orb", None),
        P(None, "orb", None),
        P(),
        P(None, "orb", "aux", None),
        P(),
    )
    out_specs = P("orb", "aux")
    return jax.shard_map(
        on_device, mesh=mesh, in_specs=in_specs, out_specs=out_specs, check_vma=False
    )
```

profile of v0, /device:TPU:2, one launch (start us, length us, event | category | flops | bytes accessed | tf_op | source)
XLA Modules:
  0.0 368.9 jit_solution(9843376873879229038)
XLA Ops:
  6.5 6.3 %convolution_bitcast_fusion = bf16[256,8,16,128]{3,2,1,0:T(8,128)(2,1)} fusion(bf16[256,8,8,128]{3,2,1,0:T(8,128)(2,1)} %param.6, s32[8]{0:T(128)} %bitcast.83), kind=kOutput, calls=%fused_computation.8 | convolution fusion | flops 67108992 | bytes 12582944 | tf_op jit(solution)/shard_map/prkc,kd->prdc/dot_general | solution.py:15
  12.8 8.8 %copy.23 = bf16[256,8,16,128]{3,1,0,2:T(8,128)(2,1)} copy(bf16[256,8,16,128]{3,2,1,0:T(8,128)(2,1)} %convolution_bitcast_fusion) | data formatting | bytes 16777216 | tf_op jit(solution)/shard_map/prkc,kd->prdc/transpose | solution.py:15
  21.6 0.0 copy-start.1
  21.6 0.0 copy-start.2
  21.6 0.0 copy-start.3
  21.6 0.0 copy-start.4
  21.6 7.6 %all-to-all-start = ((bf16[256,8,16,128]{3,1,0,2:T(8,128)(2,1)}), bf16[256,8,16,128]{3,1,0,2:T(8,128)(2,1)}, u32[]{:S(2)}, u32[]{:S(2)}) async-start(bf16[256,8,16,128]{3,1,0,2:T(8,128)(2,1)} %copy.23), calls=%async_computation | async-start | bytes 16777216 | tf_op jit(solution)/shard_map/all_to_all | solution.py:23
  29.2 0.0 all-reduce.2.cloned.1.call-start
  29.3 0.0 copy-done.1
  29.3 0.1 copy.25
  29.4 0.1 copy.26
  29.5 0.0 copy-done.2
  29.5 137.6 %all_gather.6 = bf16[2,128,128]{2,1,0:T(8,128)(2,1)S(1)} all-gather(bf16[2,8,128]{2,1,0:T(8,128)(2,1)S(1)} %copy-done.2), channel_id=1, replica_groups=mesh['orb'=16,'aux'=16] {'orb'}, dimensions={1}, use_global_device_ids=true | all-gather | bytes 69632 | tf_op jit(solution)/shard_map/all_gather | solution.py:16
  167.1 0.0 copy-done.3
  167.2 20.1 %all_gather.7 = bf16[2,1,128,128]{3,2,1,0:T(8,128)(2,1)S(1)} all-gather(bf16[2,1,8,128]{3,2,1,0:T(8,128)(2,1)S(1)} %copy-done.3), channel_id=1, replica_groups=mesh['orb'=16,'aux'=16] {'aux'}, dimensions={2}, use_global_device_ids=true | all-gather | bytes 69632 | tf_op jit(solution)/shard_map/all_gather | solution.py:22
  187.3 0.0 copy-done.4
  187.3 0.6 fusion.31
  187.9 0.0 all-to-all-done
  187.9 9.0 %copy.34 = bf16[256,8,16,128]{3,1,2,0:T(8,128)(2,1)} copy(bf16[256,8,16,128]{3,1,0,2:T(8,128)(2,1)} %all-to-all-done) | data formatting | bytes 16777216 | tf_op jit(solution)/shard_map/all_to_all | solution.py:23
  196.9 0.0 copy-start
  196.9 9.1 %convolution_convert_fusion = bf16[32768,128]{1,0:T(8,128)(2,1)} fusion(bf16[32768,128]{1,0:T(8,128)(2,1)} %bitcast.78, bf16[2,1,128,128]{3,2,1,0:T(8,128)(2,1)S(1)} %all_gather.7), kind=kOutput, calls=%fused_computation | convolution fusion | flops 1077936128 | bytes 16809984 | tf_op jit(solution)/shard_map/dot_general | solution.py:28
  206.0 0.0 copy-done
  206.0 4.5 %convolution_convert_fusion.1 = bf16[32768,128]{1,0:T(8,128)(2,1)} fusion(bf16[32768,128]{1,0:T(8,128)(2,1)S(1)} %bitcast.80, bf16[2,1,128,128]{3,2,1,0:T(8,128)(2,1)S(1)} %all_gather.7), kind=kOutput, calls=%fused_computation.1 | convolution fusion | flops 1077936128 | bytes 16809984 | tf_op jit(solution)/shard_map/dot_general | solution.py:28
  210.5 11.8 %copy.30 = bf16[256,128,128]{1,0,2:T(8,128)(2,1)} copy(bf16[256,128,128]{2,1,0:T(8,128)(2,1)} %bitcast.82) | data formatting | bytes 16777216 | tf_op jit(solution)/shard_map/reshape | solution.py:33
  222.3 11.8 %copy.27 = bf16[256,128,128]{1,0,2:T(8,128)(2,1)} copy(bf16[256,128,128]{2,1,0:T(8,128)(2,1)} %bitcast.79) | data formatting | bytes 16777216 | tf_op jit(solution)/shard_map/reshape | solution.py:23
  234.1 12.3 %copy.28 = bf16[256,128,128]{1,0,2:T(8,128)(2,1)} copy(bf16[256,128,128]{2,1,0:T(8,128)(2,1)} %bitcast.81) | data formatting | bytes 16777216 | tf_op jit(solution)/shard_map/reshape | solution.py:33
  246.4 11.0 %fusion.16 = f32[256,256]{1,0:T(8,128)S(1)} fusion(bf16[256,128,128]{1,0,2:T(8,128)(2,1)} %copy.30, bf16[256,128,128]{1,0,2:T(8,128)(2,1)} %copy.27, f32[]{:T(128)} %bitcast.18, bf16[2,128,128]{2,1,0:T(8,128)(2,1)S(1)} %mul.25), kind=kOutput, calls=%fused_computation.13 | convolution fusion | flops 3225485312 | bytes 17072132 | tf_op jit(solution)/shard_map/pmc,qmc->qp/dot_general | solution.py:39
  257.5 11.8 %fusion.25 = f32[256,256]{1,0:T(8,128)} fusion(f32[256,256]{1,0:T(8,128)S(1)} %fusion.16, bf16[256,128,128]{1,0,2:T(8,128)(2,1)} %copy.28, bf16[256,128,128]{1,0,2:T(8,128)(2,1)} %copy.27, f32[]{:T(128)} %bitcast, bf16[2,128,128]{2,1,0:T(8,128)(2,1)S(1)} %mul.25), kind=kOutput, calls=%fused_computation.16 | convolution fusion | flops 3225616384 | bytes 17334276 | tf_op jit(solution)/shard_map/pmc,qmc->qp/dot_general | solution.py:39
  269.3 0.0 all-reduce.2.cloned.1.call-update
  269.3 91.4 %all-reduce.2.cloned.1.call-done = f32[256,256]{1,0:T(8,128)} async-done(((f32[256,256]{1,0:T(8,128)}), f32[256,256]{1,0:T(8,128)}) %all-reduce.2.cloned.1.call-update) | async-done | bytes 262160 | tf_op jit(solution)/shard_map/psum | solution.py:44
  360.7 1.3 constant_dynamic-slice_fusion
  (4 shorter events, 0.1 us)
Async XLA Ops:
  21.6 7.7 %copy-start.1 = (s32[2,16,16]{2,1,0:T(8,128)S(1)}, s32[2,16,16]{2,1,0:T(8,128)}, u32[]{:S(2)}) copy-start(s32[2,16,16]{2,1,0:T(8,128)} %param.9) | copy-start | bytes 6148
  21.6 8.0 %copy-start.2 = (bf16[2,8,128]{2,1,0:T(8,128)(2,1)S(1)}, bf16[2,8,128]{2,1,0:T(8,128)(2,1)}, u32[]{:S(2)}) copy-start(bf16[2,8,128]{2,1,0:T(8,128)(2,1)} %param.8) | copy-start | bytes 12292
  21.6 145.6 %copy-start.3 = (bf16[2,1,8,128]{3,2,1,0:T(8,128)(2,1)S(1)}, bf16[2,1,8,128]{3,2,1,0:T(8,128)(2,1)}, u32[]{:S(2)}) copy-start(bf16[2,1,8,128]{3,2,1,0:T(8,128)(2,1)} %param.10) | copy-start | bytes 12292
  21.6 165.7 %copy-start.4 = (f32[2]{0:T(128)S(1)}, f32[2]{0:T(128)}, u32[]{:S(2)}) copy-start(f32[2]{0:T(128)} %param.11) | copy-start | bytes 28
  21.6 166.3 %all-to-all-start = ((bf16[256,8,16,128]{3,1,0,2:T(8,128)(2,1)}), bf16[256,8,16,128]{3,1,0,2:T(8,128)(2,1)}, u32[]{:S(2)}, u32[]{:S(2)}) async-start(bf16[256,8,16,128]{3,1,0,2:T(8,128)(2,1)} %copy.23), calls=%async_computation | async-start | bytes 16777216 | tf_op jit(solution)/shard_map/all_to_all | solution.py:23
  29.2 331.5 %all-reduce.2.cloned.1.call-start = ((), (), s32[]{:S(2)}) async-start(), calls=%async_computation.1 | async-start | bytes 524288 | tf_op jit(solution)/shard_map/psum | solution.py:44
  196.9 9.1 %copy-start = (bf16[256,8,16,128]{3,1,2,0:T(8,128)(2,1)S(1)}, bf16[256,8,16,128]{3,1,2,0:T(8,128)(2,1)}, u32[]{:S(2)}) copy-start(bf16[256,8,16,128]{3,1,2,0:T(8,128)(2,1)} %copy.34) | copy-start | bytes 25165828
Sparse Core Ops, SparseCore 0:
  269.4 91.2 all-reduce.1
where the time goes:
time: 370 us; the launch traced here: 369 us
  blocking collectives  158 us (43%)
  waiting for transfers between devices  91.4 us (25%)
  local copies, waits for them, and re-layouts  55.9 us (15%)
  matrix products  42.7 us (12%)
  between operations  13.5 us (4%)
  starting transfers between devices  7.66 us (2%)
    all_gather x1, blocking collectives, on_device(): occ_full = lax.all_gather(g_occ, 'orb', axis=1, tiled=True)  138 us
    psum x1, waiting for transfers between devices, on_device(): whole_sum = lax.psum(partial_value, 'orb')  91.4 us
    reshape x2, local copies, waits for them, and re-layouts, on_device(): product.astype(jnp.bfloat16).reshape(aux_dev, total_rows, tile_width)  24.1 us
    dot_general x2, matrix products, on_device(): jnp.einsum('pmc,qmc->qp', virt_list[moment], occ_prod, preferred_element_...  22.9 us
    all_gather x1, blocking collectives, on_device(): virt_block = lax.all_gather(g_virt, 'aux', axis=2, tiled=True)  20.1 us
    dot_general x2, matrix products, on_device(): jnp.dot(col_dense.reshape(aux_dev * total_rows, tile_width), virt_block[m...  13.6 us
    reshape x1, local copies, waits for them, and re-layouts, on_device(): lax.all_to_all(outgoing, 'orb', split_axis=2, concat_axis=1, tiled=True)  11.8 us
    all_to_all x1, local copies, waits for them, and re-layouts, on_device(): lax.all_to_all(outgoing, 'orb', split_axis=2, concat_axis=1, tiled=True)  9.03 us
  transfers between devices with their start and end apart: 2, of which 1 were waited for; matrix products, arithmetic and copies ran while one was open for 0% of the time, Pallas kernels for 0%

commit v1 on v0

--- a/solution.py
+++ b/solution.py
@@ -3,6 +3,13 @@
 import jax.numpy as jnp
 from jax import lax
 from jax.sharding import PartitionSpec as P
+
+
+def stacked_exchange(block, axis, split, join):
+    peers = lax.axis_size(axis)
+    tiles = jnp.stack(jnp.split(block, peers, axis=split), axis=0)
+    tiles = lax.all_to_all(tiles, axis, split_axis=0, concat_axis=0)
+    return jnp.concatenate(tiles, axis=join)
 
 
 def on_device(b_rows, col_blocks, g_occ, occ_live, g_virt, tau_weight):
@@ -20,9 +27,7 @@
     )
     occ_masked = occ_full * live_mask
     virt_block = lax.all_gather(g_virt, "aux", axis=2, tiled=True)
-    col_dense = lax.all_to_all(outgoing, "orb", split_axis=2, concat_axis=1, tiled=True).reshape(
-        aux_dev, total_rows, tile_width
-    )
+    col_dense = stacked_exchange(outgoing, "orb", 2, 1).reshape(aux_dev, total_rows, tile_width)
     virt_list = []
     for moment in range(tau_count):
         product = jnp.dot(

time: 370 us -> 392 us (1.059)
  local copies, waits for them, and re-layouts: 55.9 us -> 84.5 us
  matrix products: 42.7 us -> 36.2 us
    another operation x0 -> x3, local copies, waits for them, and re-layouts: none -> 20.6 us  [the longest x2 19.6 us: on_device(): stacked_exchange(outgoing, 'orb', 2, 1)]
    unnamed x10 -> x37, local copies, waits for them, and re-layouts: 0.02 us -> 19.8 us
    split x0 -> x1, local copies, waits for them, and re-layouts: none -> 17.9 us  [stacked_exchange(): tiles = jnp.stack(jnp.split(block, peers, axis=split), axis=0)]
    reshape x1 -> x0, local copies, waits for them, and re-layouts: 11.8 us -> none  [on_device(): lax.all_to_all(outgoing, 'orb', split_axis=2, concat_axis=1, tiled=True)]
    all_to_all x1 -> x0, local copies, waits for them, and re-layouts: 9.03 us -> none  [on_device(): lax.all_to_all(outgoing, 'orb', split_axis=2, concat_axis=1, tiled=True)]
    transpose x1 -> x0, local copies, waits for them, and re-layouts: 8.77 us -> none  [on_device(): outgoing = jnp.einsum('prkc,kd->prdc', b_rows, picked)]
    dot_general x2, matrix products: 13.6 us -> 8.94 us  [on_device(): jnp.dot(col_dense.reshape(aux_dev * total_rows, tile_width), virt_block[m...]
where the time goes in v1:
time: 392 us; the launch traced here: 391 us
  blocking collectives  158 us (40%)
  waiting for transfers between devices  91.4 us (23%)
  local copies, waits for them, and re-layouts  84.5 us (22%)
  matrix products  36.2 us (9%)
  between operations  13.6 us (3%)
  starting transfers between devices  7.66 us (2%)
    all_gather x1, blocking collectives, on_device(): occ_full = lax.all_gather(g_occ, 'orb', axis=1, tiled=True)  138 us
    psum x1, waiting for transfers between devices, on_device(): whole_sum = lax.psum(partial_value, 'orb')  91.4 us
    reshape x2, local copies, waits for them, and re-layouts, on_device(): product.astype(jnp.bfloat16).reshape(aux_dev, total_rows, tile_width)  24 us
    dot_general x2, matrix products, on_device(): jnp.einsum('pmc,qmc->qp', virt_list[moment], occ_prod, preferred_element_...  22.9 us
    all_gather x1, blocking collectives, on_device(): virt_block = lax.all_gather(g_virt, 'aux', axis=2, tiled=True)  20.1 us
    unnamed x37, local copies, waits for them, and re-layouts  19.8 us
    another operation x2, local copies, waits for them, and re-layouts, on_device(): stacked_exchange(outgoing, 'orb', 2, 1)  19.6 us
    split x1, local copies, waits for them, and re-layouts, stacked_exchange(): tiles = jnp.stack(jnp.split(block, peers, axis=split), axis=0)  17.9 us
  transfers between devices with their start and end apart: 2, of which 1 were waited for; matrix products, arithmetic and copies ran while one was open for 0% of the time, Pallas kernels for 0%

profile of v1, /device:TPU:2, one launch (start us, length us, event | category | flops | bytes accessed | tf_op | source)
XLA Modules:
  0.0 391.2 jit_solution(15709180875748478480)
XLA Ops:
  6.5 4.3 %convolution_bitcast_fusion = bf16[256,8,16,128]{3,2,1,0:T(8,128)(2,1)S(1)} fusion(bf16[256,8,8,128]{3,2,1,0:T(8,128)(2,1)} %param.6, s32[8]{0:T(128)} %bitcast.111), kind=kOutput, calls=%fused_computation.8 | convolution fusion | flops 67108992 | bytes 12582944 | tf_op jit(solution)/shard_map/prkc,kd->prdc/dot_general | solution.py:22
  10.9 17.9 %fusion.31 = (bf16[256,8,1,128]{3,2,1,0:T(2,128)(2,1)S(1)}, bf16[256,8,1,128]{3,2,1,0:T(2,128)(2,1)S(1)}, bf16[256,8,1,128]{3,2,1,0:T(2,128)(2,1)S(1)}, bf16[256...) fusion(bf16[256,8,16,128]{3,2,1,0:T(8,128)(2,1)S(1)} %convoluti, ...), kind=kLoop, calls=%fused_computation.44 | loop fusion | bytes 16777216 | tf_op jit(solution)/shard_map/split | solution.py:10
  28.9 2.2 bitcast_dynamic-update-slice_fusion.15
  31.2 2.5 bitcast_dynamic-update-slice_fusion.14
  33.6 2.1 bitcast_dynamic-update-slice_fusion.13
  35.7 2.1 bitcast_dynamic-update-slice_fusion.12
  37.8 2.1 bitcast_dynamic-update-slice_fusion.11
  40.0 0.9 bitcast_dynamic-update-slice_fusion.10
  40.8 0.9 bitcast_dynamic-update-slice_fusion.9
  41.7 0.9 bitcast_dynamic-update-slice_fusion.8
  42.6 0.9 bitcast_dynamic-update-slice_fusion.7
  43.5 0.9 bitcast_dynamic-update-slice_fusion.6
  44.3 0.9 bitcast_dynamic-update-slice_fusion.5
  45.2 0.9 bitcast_dynamic-update-slice_fusion.4
  46.1 0.9 bitcast_dynamic-update-slice_fusion.3
  47.0 0.9 bitcast_dynamic-update-slice_fusion.2
  47.9 0.9 bitcast_dynamic-update-slice_fusion.1
  48.7 0.9 bitcast_dynamic-update-slice_fusion
  49.7 7.6 %all-to-all-start = ((bf16[16,256,8,1,128]{4,2,1,3,0:T(8,128)(2,1)}), bf16[16,256,8,1,128]{4,2,1,3,0:T(8,128)(2,1)}, u32[]{:S(2)}, u32[]{:S(2)}) async-start(bf16[16,256,8,1,128]{4,2,1,3,0:T(8,128)(2,1)} %bitcast_dynamic-update-slice_fusion), calls=%async_computation | async-start | bytes 16777216 | tf_op jit(solution)/shard_map/all_to_all | solution.py:11
  57.6 137.6 %all_gather.6 = bf16[2,128,128]{2,1,0:T(8,128)(2,1)S(1)} all-gather(bf16[2,8,128]{2,1,0:T(8,128)(2,1)S(1)} %copy-done.8), channel_id=1, replica_groups=mesh['orb'=16,'aux'=16] {'orb'}, dimensions={1}, use_global_device_ids=true | all-gather | bytes 69632 | tf_op jit(solution)/shard_map/all_gather | solution.py:23
  195.2 20.1 %all_gather.7 = bf16[2,1,128,128]{3,2,1,0:T(8,128)(2,1)S(1)} all-gather(bf16[2,1,8,128]{3,2,1,0:T(8,128)(2,1)S(1)} %copy-done.9), channel_id=1, replica_groups=mesh['orb'=16,'aux'=16] {'aux'}, dimensions={2}, use_global_device_ids=true | all-gather | bytes 69632 | tf_op jit(solution)/shard_map/all_gather | solution.py:29
  215.4 0.7 fusion.32
  216.1 7.8 %copy_bitcast_fusion = (bf16[256,128,128]{2,1,0:T(8,128)(2,1)}, bf16[256,16,8,1,128]{4,2,1,0,3:T(8,128)(2,1)S(1)}) fusion(bf16[16,256,8,1,128]{4,2,1,3,0:T(8,128)(2,1)} %all-to-all-done), kind=kLoop, calls=%fused_computation.43 | loop fusion | bytes 25165824 | tf_op jit(solution)/shard_map/reshape;reshape | solution.py:30
  223.9 4.5 %convolution_convert_fusion = bf16[32768,128]{1,0:T(8,128)(2,1)} fusion(bf16[32768,128]{1,0:T(8,128)(2,1)S(1)} %bitcast.107, bf16[2,1,128,128]{3,2,1,0:T(8,128)(2,1)S(1)} %all_gather.7), kind=kOutput, calls=%fused_computation | convolution fusion | flops 1077936128 | bytes 16809984 | tf_op jit(solution)/shard_map/dot_general | solution.py:33
  228.3 4.5 %convolution_convert_fusion.1 = bf16[32768,128]{1,0:T(8,128)(2,1)} fusion(bf16[32768,128]{1,0:T(8,128)(2,1)S(1)} %bitcast.108, bf16[2,1,128,128]{3,2,1,0:T(8,128)(2,1)S(1)} %all_gather.7), kind=kOutput, calls=%fused_computation.1 | convolution fusion | flops 1077936128 | bytes 16809984 | tf_op jit(solution)/shard_map/dot_general | solution.py:33
  232.8 11.8 %copy.254 = bf16[256,128,128]{1,0,2:T(8,128)(2,1)} copy(bf16[256,128,128]{2,1,0:T(8,128)(2,1)} %bitcast.110) | data formatting | bytes 16777216 | tf_op jit(solution)/shard_map/reshape | solution.py:38
  244.6 11.8 %copy.250 = bf16[256,128,128]{1,0,2:T(8,128)(2,1)} copy(bf16[256,128,128]{2,1,0:T(8,128)(2,1)} %get-tuple-element.5) | data formatting | bytes 16777216 | tf_op jit(solution)/shard_map/reshape;reshape | solution.py:30
  256.4 12.2 %copy.252 = bf16[256,128,128]{1,0,2:T(8,128)(2,1)} copy(bf16[256,128,128]{2,1,0:T(8,128)(2,1)} %bitcast.109) | data formatting | bytes 16777216 | tf_op jit(solution)/shard_map/reshape | solution.py:38
  268.6 11.1 %fusion.16 = f32[256,256]{1,0:T(8,128)S(1)} fusion(bf16[256,128,128]{1,0,2:T(8,128)(2,1)} %copy.254, bf16[256,128,128]{1,0,2:T(8,128)(2,1)} %copy.250, f32[]{:T(128)} %bitcast.16, bf16[2,128,128]{2,1,0:T(8,128)(2,1)S(1)} %mul.25), kind=kOutput, calls=%fused_computation.13 | convolution fusion | flops 3225485312 | bytes 17072132 | tf_op jit(solution)/shard_map/pmc,qmc->qp/dot_general | solution.py:44
  279.7 11.8 %fusion.25 = f32[256,256]{1,0:T(8,128)} fusion(f32[256,256]{1,0:T(8,128)S(1)} %fusion.16, bf16[256,128,128]{1,0,2:T(8,128)(2,1)} %copy.252, bf16[256,128,128]{1,0,2:T(8,128)(2,1)} %copy.250, f32[]{:T(128)} %bitcast, bf16[2,128,128]{2,1,0:T(8,128)(2,1)S(1)} %mul.25), kind=kOutput, calls=%fused_computation.16 | convolution fusion | flops 3225616384 | bytes 17334276 | tf_op jit(solution)/shard_map/pmc,qmc->qp/dot_general | solution.py:44
  291.6 91.4 %all-reduce.2.cloned.1.call-done = f32[256,256]{1,0:T(8,128)} async-done(((f32[256,256]{1,0:T(8,128)}), f32[256,256]{1,0:T(8,128)}) %all-reduce.2.cloned.1.call-update) | async-done | bytes 262160 | tf_op jit(solution)/shard_map/psum | solution.py:49
  383.0 1.3 constant_dynamic-slice_fusion
  (31 shorter events, 0.4 us)
Async XLA Ops:
  28.8 11.1 %copy-start.6 = (bf16[256,8,1,128]{3,2,1,0:T(2,128)(2,1)S(1)}, bf16[256,8,1,128]{3,2,1,0:T(2,128)(2,1)}, u32[]{:S(2)}) copy-start(bf16[256,8,1,128]{3,2,1,0:T(2,128)(2,1)} %get-tuple-element.17) | copy-start | bytes 1572868
  28.9 12.0 %copy-start.5 = (bf16[256,8,1,128]{3,2,1,0:T(2,128)(2,1)S(1)}, bf16[256,8,1,128]{3,2,1,0:T(2,128)(2,1)}, u32[]{:S(2)}) copy-start(bf16[256,8,1,128]{3,2,1,0:T(2,128)(2,1)} %get-tuple-element.16) | copy-start | bytes 1572868
  28.9 12.8 %copy-start.4 = (bf16[256,8,1,128]{3,2,1,0:T(2,128)(2,1)S(1)}, bf16[256,8,1,128]{3,2,1,0:T(2,128)(2,1)}, u32[]{:S(2)}) copy-start(bf16[256,8,1,128]{3,2,1,0:T(2,128)(2,1)} %get-tuple-element.15) | copy-start | bytes 1572868
  28.9 13.7 %copy-start.3 = (bf16[256,8,1,128]{3,2,1,0:T(2,128)(2,1)S(1)}, bf16[256,8,1,128]{3,2,1,0:T(2,128)(2,1)}, u32[]{:S(2)}) copy-start(bf16[256,8,1,128]{3,2,1,0:T(2,128)(2,1)} %get-tuple-element.14) | copy-start | bytes 1572868
  28.9 14.6 %copy-start.2 = (bf16[256,8,1,128]{3,2,1,0:T(2,128)(2,1)S(1)}, bf16[256,8,1,128]{3,2,1,0:T(2,128)(2,1)}, u32[]{:S(2)}) copy-start(bf16[256,8,1,128]{3,2,1,0:T(2,128)(2,1)} %get-tuple-element.13) | copy-start | bytes 1572868
  28.9 15.4 %copy-start.1 = (bf16[256,8,1,128]{3,2,1,0:T(2,128)(2,1)S(1)}, bf16[256,8,1,128]{3,2,1,0:T(2,128)(2,1)}, u32[]{:S(2)}) copy-start(bf16[256,8,1,128]{3,2,1,0:T(2,128)(2,1)} %get-tuple-element.12) | copy-start | bytes 1572868
  28.9 16.3 %copy-start = (bf16[256,8,1,128]{3,2,1,0:T(2,128)(2,1)S(1)}, bf16[256,8,1,128]{3,2,1,0:T(2,128)(2,1)}, u32[]{:S(2)}) copy-start(bf16[256,8,1,128]{3,2,1,0:T(2,128)(2,1)} %get-tuple-element.11) | copy-start | bytes 1572868
  49.7 7.7 %copy-start.7 = (s32[2,16,16]{2,1,0:T(8,128)S(1)}, s32[2,16,16]{2,1,0:T(8,128)}, u32[]{:S(2)}) copy-start(s32[2,16,16]{2,1,0:T(8,128)} %param.9) | copy-start | bytes 6148
  49.7 8.0 %copy-start.8 = (bf16[2,8,128]{2,1,0:T(8,128)(2,1)S(1)}, bf16[2,8,128]{2,1,0:T(8,128)(2,1)}, u32[]{:S(2)}) copy-start(bf16[2,8,128]{2,1,0:T(8,128)(2,1)} %param.8) | copy-start | bytes 12292
  49.7 145.6 %copy-start.9 = (bf16[2,1,8,128]{3,2,1,0:T(8,128)(2,1)S(1)}, bf16[2,1,8,128]{3,2,1,0:T(8,128)(2,1)}, u32[]{:S(2)}) copy-start(bf16[2,1,8,128]{3,2,1,0:T(8,128)(2,1)} %param.10) | copy-start | bytes 12292
  49.7 165.7 %copy-start.10 = (f32[2]{0:T(128)S(1)}, f32[2]{0:T(128)}, u32[]{:S(2)}) copy-start(f32[2]{0:T(128)} %param.11) | copy-start | bytes 28
  49.7 166.4 %all-to-all-start = ((bf16[16,256,8,1,128]{4,2,1,3,0:T(8,128)(2,1)}), bf16[16,256,8,1,128]{4,2,1,3,0:T(8,128)(2,1)}, u32[]{:S(2)}, u32[]{:S(2)}) async-start(bf16[16,256,8,1,128]{4,2,1,3,0:T(8,128)(2,1)} %bitcast_dynamic-update-slice_fusion), calls=%async_computation | async-start | bytes 16777216 | tf_op jit(solution)/shard_map/all_to_all | solution.py:11
  57.3 325.7 %all-reduce.2.cloned.1.call-start = ((), (), s32[]{:S(2)}) async-start(), calls=%async_computation.1 | async-start | bytes 524288 | tf_op jit(solution)/shard_map/psum | solution.py:49
Sparse Core Ops, SparseCore 0:
  291.7 91.2 all-reduce.1
